TPU v7x, 32 devices: a whole 2x2x4 slice. The times are simulated.
32 devices in a mesh: lat: 4 (over y, core), lon: 8 (over z, x).
Axes of the slice: x: 2, y: 2, z: 4, core: 2. Of those that a mesh axis runs over, the one named last changes fastest.
Arguments:
- control: bfloat16 [80, 32, 64, 512], P(None, None, 'lon', 'lat'), may hold values from -6 to 6
- ensemble: bfloat16 [80, 32, 64, 512], P(None, None, 'lon', 'lat'), may hold values from -1.1953125 to 1.1953125
- level_mix: bfloat16 [32, 32], replicated, may hold values from -1 to 1
- lat_taps: float32 [4], replicated, may hold values from 0.1 to 0.6
- lon_taps: float32 [4], replicated, may hold values from 0.1 to 0.6
- obs_location: int32 [8, 4, 2048], P('lon', 'lat'), may hold values from 0 to 32767
- obs_count: int32 [8, 4], P('lon', 'lat'), may hold values from 512 to 2048, as said below
- obs_keep: int32 [8, 4, 2048], P('lon', 'lat'), may hold values 0 or 1
- innovation: float32 [8, 4, 2048], P('lon', 'lat'), may hold values from -6 to 6
- obs_weight: float32 [8, 4, 2048], P('lon', 'lat'), may hold values from 0.25 to 4
Outputs:
- gradient: float32 [80, 32, 64, 512], P(None, None, 'lon', 'lat')
- upper_factor: float32 [80, 80], replicated
Inputs may be any that keep to these rules, and one draw needn't show every extreme that they name: `obs_count`: live slots of a tile come first; some tile has all 2048 slots live.
All inputs are finite; a program needn't handle non-finite values. No bound on the sum of `obs_keep` on one device may be relied on, other than what follows from the above.
Results may differ from a plain program's by a relative error of at most 0.0028.
Values may be sent and summed in bfloat16 or wider, within the bound.
A program may use at most 128 MiB of HBM per device.

v0:
```python
import jax
import jax.numpy as jnp
from jax import lax
from jax.sharding import PartitionSpec as P

OFFSETS = (-2, -1, 1, 2)


def with_halo(shard, sides, width, wrap):
    for axis, dim in sides:
        size, length = (lax.axis_size(axis), shard.shape[dim])
        up = [(i, (i + 1) % size) for i in range(size if wrap else size - 1)]
        down = [(j, i) for i, j in up]
        last = lax.slice_in_dim(shard, length - width, length, axis=dim)
        leading = lax.slice_in_dim(shard, 0, width, axis=dim)
        before = lax.ppermute(last, axis, up)
        after = lax.ppermute(leading, axis, down)
        shard = jnp.concatenate([before, shard, after], axis=dim)
    return shard


def taps_along(padded, weights, dimension, direction, extent):
    summed = lax.slice_in_dim(padded, 2, 2 + extent, axis=dimension).astype(jnp.float32)
    for position in range(4):
        begin_at = 2 + direction * OFFSETS[position]
        piece = lax.slice_in_dim(padded, begin_at, begin_at + extent, axis=dimension)
        summed = summed + weights[position] * piece.astype(jnp.float32)
    return summed


def shards(
    control,
    ensemble,
    level_mix,
    lat_taps,
    lon_taps,
    obs_location,
    obs_count,
    obs_keep,
    innovation,
    obs_weight,
):
    members, levels, lon_cells, lat_cells = control.shape
    mixed_levels = jnp.einsum(
        "kl,mlab->mkab", level_mix, control, preferred_element_type=jnp.float32
    ).astype(jnp.bfloat16)
    padded = with_halo(mixed_levels, (("lat", 3),), 2, False)
    rowwise = taps_along(padded, lat_taps, 3, 1, lat_cells)
    widened = with_halo(rowwise, (("lon", 2),), 2, True)
    localized = taps_along(widened, lon_taps, 2, 1, lon_cells)
    increment = jnp.sum(ensemble.astype(jnp.float32) * localized, axis=0)
    places = obs_location[0, 0]
    slot_ids = jnp.arange(places.shape[0], dtype=jnp.int32)
    live_slots = (slot_ids < obs_count[0, 0]).astype(jnp.float32) * obs_keep[0, 0].astype(
        jnp.float32
    )
    weights = live_slots * obs_weight[0, 0]
    flat_inc = increment.reshape(-1)
    misfit = weights * (flat_inc[places] - innovation[0, 0])
    pulled = jnp.zeros_like(flat_inc).at[places].add(misfit).reshape(increment.shape)
    pulled_members = (ensemble.astype(jnp.float32) * pulled[None]).astype(jnp.bfloat16)
    padded_back = with_halo(pulled_members, (("lon", 2),), 2, True)
    colwise = taps_along(padded_back, lon_taps, 2, -1, lon_cells)
    tall_block = with_halo(colwise, (("lat", 3),), 2, False)
    spread = taps_along(tall_block, lat_taps, 3, -1, lat_cells)
    mixed_back = jnp.einsum(
        "kl,mkab->mlab", level_mix, spread.astype(jnp.bfloat16), preferred_element_type=jnp.float32
    )
    gradient = control.astype(jnp.float32) + mixed_back
    columns = ensemble.reshape(members, -1)[:, places]
    scaled = columns.astype(jnp.float32) * jnp.sqrt(weights)[None, :]
    local_gram = jnp.dot(scaled, scaled.T, precision=lax.Precision.HIGHEST)
    tiles_all = lax.axis_size("lat") * lax.axis_size("lon")
    total_obs = places.shape[0] * tiles_all
    identity = jnp.eye(members, dtype=jnp.float32)
    summed_gram = lax.psum(local_gram, ("lat", "lon"))
    upper_factor = jnp.linalg.cholesky(identity + members / total_obs * summed_gram).T
    return (gradient, upper_factor)


def solution(mesh):
    in_specs = (
        P(None, None, "lon", "lat"),
        P(None, None, "lon", "lat"),
        P(),
        P(),
        P(),
        P("lon", "lat", None),
        P("lon", "lat"),
        P("lon", "lat", None),
        P("lon", "lat", None),
        P("lon", "lat", None),
    )
    out_specs = (P(None, None, "lon", "lat"), P())
    return jax.shard_map(shards, mesh=mesh, in_specs=in_specs, out_specs=out_specs, check_vma=False)
```

profile of v0, /device:TPU:1, one launch (start us, length us, event | category | flops | bytes accessed | tf_op | source)
XLA Modules:
  0.0 486.5 jit_solution(9345131680365541441)
XLA Ops:
  1.3 6.4 %convert_bitcast_fusion = bf16[80,32,8,128]{3,1,2,0:T(8,128)(2,1)} fusion(bf16[80,32,8,128]{3,2,1,0:T(8,128)(2,1)} %param.10, bf16[32,32]{1,0:T(8,128)(2,1)S(1)} %copy-done), kind=kOutput, calls=%fused_computation.59 | convolution fusion | flops 170393600 | bytes 10487808 | tf_op jit(solution)/shard_map/kl,mlab->mkab/dot_general | solution.py:44
  7.7 11.1 %fusion.49 = (bf16[80,32,8,2]{3,1,2,0:T(8,128)(2,1)}, bf16[80,32,8,2]{3,1,2,0:T(8,128)(2,1)}) fusion(bf16[80,32,8,128]{3,1,2,0:T(8,128)(2,1)} %convert_bitcast_fusion), kind=kLoop, calls=%fused_computation.90 | loop fusion | bytes 327680 | tf_op jit(solution)/shard_map/slice | solution.py:14
  18.8 7.6 %copy.57 = bf16[80,32,8,2]{0,2,3,1:T(8,128)(2,1)S(1)} copy(bf16[80,32,8,2]{3,1,2,0:T(8,128)(2,1)} %get-tuple-element.17) | data formatting | bytes 163840 | tf_op jit(solution)/shard_map/slice | solution.py:15
  28.3 7.5 %copy.55 = bf16[80,32,8,2]{0,2,3,1:T(8,128)(2,1)S(1)} copy(bf16[80,32,8,2]{3,1,2,0:T(8,128)(2,1)} %get-tuple-element.16) | data formatting | bytes 163840 | tf_op jit(solution)/shard_map/slice | solution.py:14
  41.2 9.3 %copy.58 = bf16[80,32,8,2]{3,1,2,0:T(8,128)(2,1)} copy(bf16[80,32,8,2]{0,2,3,1:T(8,128)(2,1)S(1)} %collective-permute-done.1) | data formatting | bytes 163840 | tf_op jit(solution)/shard_map/ppermute | solution.py:17
  50.5 9.3 %copy.56 = bf16[80,32,8,2]{3,1,2,0:T(8,128)(2,1)} copy(bf16[80,32,8,2]{0,2,3,1:T(8,128)(2,1)S(1)} %collective-permute-done) | data formatting | bytes 163840 | tf_op jit(solution)/shard_map/ppermute | solution.py:16
  59.8 30.0 %multiply_add_fusion.1 = f32[80,32,8,128]{3,1,2,0:T(8,128)S(1)} fusion(bf16[80,32,8,128]{3,1,2,0:T(8,128)(2,1)} %convert_bitcast_fusion, bf16[80,32,8,2]{3,1,2,0:T(8,128)(2,1)} %copy.58, bf16[80,32,8,2]{3,1,2,0:T(8,128)(2,1)} %copy.56, f32[]{:T(128)} %bitcast.11, f32[]{:T(128)} %bitcast.10, f32[]{:T(128)} %bitcast.9, f32[]{:T(128)} %bitcast.8), kind=kLoop, calls=%fused_computation.46 | loop fusion | flops 65536000 | bytes 15892496 | tf_op jit(solution)/shard_map/add | solution.py:27
  96.2 108.5 %collective-permute-done.3 = f32[80,32,2,128]{3,1,2,0:T(8,128)S(1)} collective-permute-done((f32[80,32,2,128]{3,1,2,0:T(8,128)S(1)}, f32[80,32,2,128]{3,1,2,0:T(8,128)S(1)}, u32[]{:S(2)}, u32[]{:S(2)}) %collective-permute-start.3) | collective-permute-done | bytes 2621472 | tf_op jit(solution)/shard_map/ppermute | solution.py:17
  206.9 11.6 %fusion = f32[32,8,128]{2,0,1:T(8,128)S(1)} fusion(f32[80,32,8,128]{3,1,2,0:T(8,128)S(1)} %multiply_add_fusion.1, f32[80,32,2,128]{3,1,2,0:T(8,128)S(1)} %collective-permute-done.3, f32[80,32,2,128]{3,1,2,0:T(8,128)} %copy-done.3, f32[]{:T(128)} %bitcast.15, f32[]{:T(128)} %bitcast.14, f32[]{:T(128)} %bitcast.13, f32[]{:T(128)} %bitcast.12, ...), kind=kLoop, calls=%fused_computation.13 | loop fusion | flops 39288832 | bytes 21102608 | tf_op jit(solution)/shard_map/reduce_sum | solution.py:51
  218.6 11.8 %gather_fusion = f32[2048]{0:T(1024)S(1)} fusion(f32[32768]{0:T(1024)S(1)} %bitcast.39, s32[2048]{0:T(1024)S(1)} %broadcast_clamp_fusion), kind=kCustom, calls=%fused_computation | custom fusion | bytes 24576 | tf_op jit(solution)/shard_map/gather | solution.py:59
  230.4 11.5 %scatter_custom_fusion = f32[32768]{0:T(1024)S(1)} fusion(s32[2048]{0:T(1024)S(1)} %bitcast.44, f32[2048]{0:T(1024)S(1)} %get-tuple-element.19, f32[]{:T(128)} %constant.39.clone.1), kind=kCustom, calls=%fused_computation.68 | custom fusion | flops 2048 | bytes 131076 | tf_op jit(solution)/shard_map/scatter-add | solution.py:60
  255.2 10.6 %copy.66 = bf16[80,32,8,128]{0,3,2,1:T(8,128)(2,1)} copy(bf16[80,32,8,128]{3,2,1,0:T(8,128)(2,1)} %param.11) | data formatting | bytes 10485760 | tf_op args[1]
  265.8 10.1 %gather_fusion.1 = bf16[2048,80]{1,0:T(8,128)(2,1)S(1)} fusion(bf16[80,32768]{0,1:T(8,128)(2,1)} %bitcast.40, s32[2048]{0:T(1024)S(1)} %broadcast_clamp_fusion), kind=kCustom, calls=%fused_computation.1 | custom fusion | bytes 663552 | tf_op jit(solution)/shard_map/gather | solution.py:70
  278.3 65.3 %psum.7 = f32[80,80]{0,1:T(8,128)S(1)} all-reduce(f32[80,80]{0,1:T(8,128)S(1)} %fusion.35), channel_id=1, replica_groups=mesh['lat'=4,'lon'=8] {'lat','lon'}, use_global_device_ids=true, to_apply=%region_2.0 | all-reduce | flops 6400 | bytes 51200 | tf_op jit(solution)/shard_map/psum | solution.py:76
  343.7 7.3 %cholesky.20 = f32[80,80]{1,0:T(8,128)S(1)} custom-call(f32[80,80]{1,0:T(8,128)S(1)} %fusion.41), custom_call_target="Cholesky" | custom-call | tf_op jit(solution)/shard_map/jit(cholesky)/cholesky | solution.py:77
  351.8 13.8 %multiply_add_fusion = f32[80,32,8,128]{3,1,2,0:T(8,128)S(1)} fusion(bf16[80,32,8,128]{3,1,2,0:T(8,128)(2,1)} %copy-done.2, bf16[80,32,2,128]{3,1,2,0:T(8,128)(2,1)S(1)} %collective-permute-done.5, bf16[80,32,2,128]{3,1,2,0:T(8,128)(2,1)S(1)} %collective-permute-done.4, f32[]{:T(128)} %bitcast.15, f32[]{:T(128)} %bitcast.14, f32[]{:T(128)} %bitcast.13, ...), kind=kLoop, calls=%fused_computation.45 | loop fusion | flops 44564480 | bytes 18350096 | tf_op jit(solution)/shard_map/add | solution.py:27
  365.7 9.6 %fusion.46 = (f32[80,32,8,2]{3,1,2,0:T(8,128)}, f32[80,32,8,2]{3,1,2,0:T(8,128)}) fusion(f32[80,32,8,128]{3,1,2,0:T(8,128)S(1)} %multiply_add_fusion), kind=kLoop, calls=%fused_computation.87 | loop fusion | bytes 655360 | tf_op jit(solution)/shard_map/slice | solution.py:15
  375.9 7.5 %copy.63 = f32[80,32,8,2]{0,2,3,1:T(8,128)S(1)} copy(f32[80,32,8,2]{3,1,2,0:T(8,128)} %get-tuple-element.11) | data formatting | bytes 327680 | tf_op jit(solution)/shard_map/slice | solution.py:14
  383.4 5.6 %collective-permute-start.7 = (f32[80,32,8,2]{0,2,3,1:T(8,128)S(1)}, f32[80,32,8,2]{0,2,3,1:T(8,128)S(1)}, u32[]{:S(2)}, u32[]{:S(2)}) collective-permute-start(f32[80,32,8,2]{0,2,3,1:T(8,128)S(1)} %copy.63), channel_id=1, source_target_pairs={{0,8},{8,16},{16,24},{1,9},{9,17},{17,25},{2,10},{10,18},{18,26},{... | collective-permute-start | bytes 491528 | tf_op jit(solution)/shard_map/ppermute | solution.py:16
  389.0 7.5 %copy.61 = f32[80,32,8,2]{0,2,3,1:T(8,128)S(1)} copy(f32[80,32,8,2]{3,1,2,0:T(8,128)} %get-tuple-element.10) | data formatting | bytes 327680 | tf_op jit(solution)/shard_map/slice | solution.py:15
  399.7 9.1 %copy.64 = f32[80,32,8,2]{3,1,2,0:T(8,128)} copy(f32[80,32,8,2]{0,2,3,1:T(8,128)S(1)} %collective-permute-done.7) | data formatting | bytes 327680 | tf_op jit(solution)/shard_map/ppermute | solution.py:16
  408.8 9.2 %copy.62 = f32[80,32,8,2]{3,1,2,0:T(8,128)} copy(f32[80,32,8,2]{0,2,3,1:T(8,128)S(1)} %collective-permute-done.6) | data formatting | bytes 327680 | tf_op jit(solution)/shard_map/ppermute | solution.py:17
  418.0 49.9 %bitcast_add_fusion = f32[80,32,8,128]{3,1,2,0:T(8,128)} fusion(bf16[80,32,8,128]{3,2,1,0:T(8,128)(2,1)} %param.10, f32[80,32,8,2]{3,1,2,0:T(8,128)} %copy.64, f32[80,32,8,128]{3,1,2,0:T(8,128)} %copy-done.1, f32[80,32,8,2]{3,1,2,0:T(8,128)} %copy.62, f32[]{:T(128)} %bitcast.11, f32[]{:T(128)} %bitcast.10, f32[]{:T(128)} %bitcast.9, f32[]{:T(128)} %bitcast.8, ...), kind=kOutput, calls=%fused_computation.44 | convolution fusion | flops 207093760 | bytes 26544144 | tf_op jit(solution)/shard_map/kl,mkab->mlab/dot_general | solution.py:66
  467.9 18.3 %copy.71 = f32[80,32,8,128]{3,2,1,0:T(8,128)} copy(f32[80,32,8,128]{3,1,2,0:T(8,128)} %bitcast_add_fusion) | data formatting | bytes 20971520
  (53 shorter events, 36.3 us)
Async XLA Ops:
  0.6 0.7 copy-start
  18.8 21.7 %copy-start.8 = (f32[4]{0:T(128)S(1)}, f32[4]{0:T(128)}, u32[]{:S(2)}) copy-start(f32[4]{0:T(128)} %param.13) | copy-start | bytes 52
  26.4 14.8 %collective-permute-start.1 = (bf16[80,32,8,2]{0,2,3,1:T(8,128)(2,1)S(1)}, bf16[80,32,8,2]{0,2,3,1:T(8,128)(2,1)S(1)}, u32[]{:S(2)}, u32[]{:S(2)}) collective-permute-start(bf16[80,32,8,2]{0,2,3,1:T(8,128)(2,1)S(1)} %copy.57), channel_id=1, source_target_pairs={{8,0},{16,8},{24,16},{9,1},{17,9},{25,17},{10,2},{18,10},{26,18},{... | collective-permute-start | bytes 245768 | tf_op jit(solution)/shard_map/ppermute | solution.py:17
  35.9 14.6 %collective-permute-start = (bf16[80,32,8,2]{0,2,3,1:T(8,128)(2,1)S(1)}, bf16[80,32,8,2]{0,2,3,1:T(8,128)(2,1)S(1)}, u32[]{:S(2)}, u32[]{:S(2)}) collective-permute-start(bf16[80,32,8,2]{0,2,3,1:T(8,128)(2,1)S(1)} %copy.55), channel_id=1, source_target_pairs={{0,8},{8,16},{16,24},{1,9},{9,17},{17,25},{2,10},{10,18},{18,26},{... | collective-permute-start | bytes 245768 | tf_op jit(solution)/shard_map/ppermute | solution.py:16
  89.8 5.0 %copy-start.6 = (s32[1,1,2048]{2,1,0:T(1,128)S(1)}, s32[1,1,2048]{2,1,0:T(1,128)}, u32[]{:S(2)}) copy-start(s32[1,1,2048]{2,1,0:T(1,128)} %param.17) | copy-start | bytes 24580
  89.8 5.7 %copy-start.9 = (f32[4]{0:T(128)S(1)}, f32[4]{0:T(128)}, u32[]{:S(2)}) copy-start(f32[4]{0:T(128)} %param.14) | copy-start | bytes 52
  89.8 6.3 %copy-start.7 = (s32[1,1,2048]{2,1,0:T(1,128)S(1)}, s32[1,1,2048]{2,1,0:T(1,128)}, u32[]{:S(2)}) copy-start(s32[1,1,2048]{2,1,0:T(1,128)} %param.15) | copy-start | bytes 24580
  90.5 114.1 %collective-permute-start.3 = (f32[80,32,2,128]{3,1,2,0:T(8,128)S(1)}, f32[80,32,2,128]{3,1,2,0:T(8,128)S(1)}, u32[]{:S(2)}, u32[]{:S(2)}) collective-permute-start(f32[80,32,2,128]{3,1,2,0:T(8,128)S(1)} %get-tuple-element.13), channel_id=1, source_target_pairs={{1,0},{2,1},{3,2},{4,3},{5,4},{6,5},{7,6},{0,7},{9,8},{10,9},{11,1... | collective-permute-start | bytes 7864328 | tf_op jit(solution)/shard_map/ppermute | solution.py:17
  94.8 110.6 %collective-permute-start.2 = (f32[80,32,2,128]{3,1,2,0:T(8,128)S(1)}, f32[80,32,2,128]{3,1,2,0:T(8,128)S(1)}, u32[]{:S(2)}, u32[]{:S(2)}) collective-permute-start(f32[80,32,2,128]{3,1,2,0:T(8,128)S(1)} %get-tuple-element.12), channel_id=1, source_target_pairs={{0,1},{1,2},{2,3},{3,4},{4,5},{5,6},{6,7},{7,0},{8,9},{9,10},{10,1... | collective-permute-start | bytes 7864328 | tf_op jit(solution)/shard_map/ppermute | solution.py:16
  205.4 1.5 copy-start.3
  206.9 23.5 %copy-start.4 = (f32[1,1,2048]{2,1,0:T(1,128)S(1)}, f32[1,1,2048]{2,1,0:T(1,128)}, u32[]{:S(2)}) copy-start(f32[1,1,2048]{2,1,0:T(1,128)} %param.19) | copy-start | bytes 24580
  206.9 23.5 %copy-start.5 = (f32[1,1,2048]{2,1,0:T(1,128)S(1)}, f32[1,1,2048]{2,1,0:T(1,128)}, u32[]{:S(2)}) copy-start(f32[1,1,2048]{2,1,0:T(1,128)} %param.18) | copy-start | bytes 24580
  246.2 2.3 copy-start.2
  250.6 101.2 %collective-permute-start.5 = (bf16[80,32,2,128]{3,1,2,0:T(8,128)(2,1)}, bf16[80,32,2,128]{3,1,2,0:T(8,128)(2,1)S(1)}, u32[]{:S(2)}, u32[]{:S(2)}) collective-permute-start(bf16[80,32,2,128]{3,1,2,0:T(8,128)(2,1)} %get-tuple-element.15), channel_id=1, source_target_pairs={{0,1},{1,2},{2,3},{3,4},{4,5},{5,6},{6,7},{7,0},{8,9},{9,10},{10,1... | collective-permute-start | bytes 3932168 | tf_op jit(solution)/shard_map/ppermute | solution.py:16
  252.8 99.1 %collective-permute-start.4 = (bf16[80,32,2,128]{3,1,2,0:T(8,128)(2,1)}, bf16[80,32,2,128]{3,1,2,0:T(8,128)(2,1)S(1)}, u32[]{:S(2)}, u32[]{:S(2)}) collective-permute-start(bf16[80,32,2,128]{3,1,2,0:T(8,128)(2,1)} %get-tuple-element.14), channel_id=1, source_target_pairs={{1,0},{2,1},{3,2},{4,3},{5,4},{6,5},{7,6},{0,7},{9,8},{10,9},{11,1... | collective-permute-start | bytes 3932168 | tf_op jit(solution)/shard_map/ppermute | solution.py:17
  365.7 10.2 %copy-start.1 = (f32[80,32,8,128]{3,1,2,0:T(8,128)}, f32[80,32,8,128]{3,1,2,0:T(8,128)S(1)}, u32[]{:S(2)}) copy-start(f32[80,32,8,128]{3,1,2,0:T(8,128)S(1)} %multiply_add_fusion) | copy-start | bytes 31457284
  383.4 16.3 %collective-permute-start.7 = (f32[80,32,8,2]{0,2,3,1:T(8,128)S(1)}, f32[80,32,8,2]{0,2,3,1:T(8,128)S(1)}, u32[]{:S(2)}, u32[]{:S(2)}) collective-permute-start(f32[80,32,8,2]{0,2,3,1:T(8,128)S(1)} %copy.63), channel_id=1, source_target_pairs={{0,8},{8,16},{16,24},{1,9},{9,17},{17,25},{2,10},{10,18},{18,26},{... | collective-permute-start | bytes 491528 | tf_op jit(solution)/shard_map/ppermute | solution.py:16
  396.5 12.3 %collective-permute-start.6 = (f32[80,32,8,2]{0,2,3,1:T(8,128)S(1)}, f32[80,32,8,2]{0,2,3,1:T(8,128)S(1)}, u32[]{:S(2)}, u32[]{:S(2)}) collective-permute-start(f32[80,32,8,2]{0,2,3,1:T(8,128)S(1)} %copy.61), channel_id=1, source_target_pairs={{8,0},{16,8},{24,16},{9,1},{17,9},{25,17},{10,2},{18,10},{26,18},{... | collective-permute-start | bytes 491528 | tf_op jit(solution)/shard_map/ppermute | solution.py:17
where the time goes:
time: 493 us; the launch traced here: 486 us
  local copies, waits for them, and re-layouts  148 us (30%)
  waiting for transfers between devices  109 us (22%)
  other arithmetic  80.5 us (16%)
  blocking collectives  65.3 us (13%)
  matrix products  58.6 us (12%)
  starting transfers between devices  23.1 us (5%)
    ppermute x4, waiting for transfers between devices, with_halo(): after = lax.ppermute(leading, axis, down)  108 us
    psum x1, blocking collectives, shards(): summed_gram = lax.psum(local_gram, ('lat', 'lon'))  65.3 us
    dot_general x1, matrix products, shards(): jnp.einsum('kl,mkab->mlab', level_mix, spread.astype(jnp.bfloat16), prefe...  49.9 us
    add x2, other arithmetic, taps_along(): summed = summed + weights[position] * piece.astype(jnp.float32)  43.9 us
    unnamed x22, local copies, waits for them, and re-layouts  34.1 us
    slice x4, local copies, waits for them, and re-layouts, with_halo(): last = lax.slice_in_dim(shard, length - width, length, axis=dim)  26.8 us
    slice x4, local copies, waits for them, and re-layouts, with_halo(): leading = lax.slice_in_dim(shard, 0, width, axis=dim)  26.7 us
    ppermute x2, local copies, waits for them, and re-layouts, with_halo(): after = lax.ppermute(leading, axis, down)  18.5 us
  transfers between devices with their start and end apart: 8, of which 2 were waited for; matrix products, arithmetic and copies ran while one was open for 14% of the time, Pallas kernels for 0%

commit v1 on v0

--- a/solution.py
+++ b/solution.py
@@ -73,7 +73,7 @@
     tiles_all = lax.axis_size("lat") * lax.axis_size("lon")
     total_obs = places.shape[0] * tiles_all
     identity = jnp.eye(members, dtype=jnp.float32)
-    summed_gram = lax.psum(local_gram, ("lat", "lon"))
+    summed_gram = jnp.sum(lax.all_gather(local_gram, ("lat", "lon")), axis=0)
     upper_factor = jnp.linalg.cholesky(identity + members / total_obs * summed_gram).T
     return (gradient, upper_factor)
 

time: 493 us -> 542 us (1.099)
  blocking collectives: 65.3 us -> 116 us
  waiting for transfers between devices: 109 us -> 88.5 us
  other arithmetic: 80.5 us -> 91.7 us
    all_gather x0 -> x1, blocking collectives: none -> 116 us  [shards(): summed_gram = jnp.sum(lax.all_gather(local_gram, ('lat', 'lon')), axis=0)]
    psum x1 -> x0, blocking collectives: 65.3 us -> none  [shards(): summed_gram = lax.psum(local_gram, ('lat', 'lon'))]
    ppermute x4, waiting for transfers between devices: 108 us -> 87.8 us  [with_halo(): after = lax.ppermute(leading, axis, down)]
    reduce_sum x1, other arithmetic: 11.6 us -> 23 us  [shards(): increment = jnp.sum(ensemble.astype(jnp.float32) * localized, axis=0)]
  transfers between devices with their start and end apart: 8 -> 8, of which waited for: 2 -> 2; matrix products, arithmetic and copies ran while one was open for 14% -> 13% of each run, Pallas kernels for 0% -> 0%
where the time goes in v1:
time: 542 us; the launch traced here: 536 us
  local copies, waits for them, and re-layouts  152 us (28%)
  blocking collectives  116 us (21%)
  other arithmetic  91.7 us (17%)
  waiting for transfers between devices  88.5 us (16%)
  matrix products  58.8 us (11%)
  starting transfers between devices  26.3 us (5%)
    all_gather x1, blocking collectives, shards(): summed_gram = jnp.sum(lax.all_gather(local_gram, ('lat', 'lon')), axis=0)  116 us
    ppermute x4, waiting for transfers between devices, with_halo(): after = lax.ppermute(leading, axis, down)  87.8 us
    dot_general x1, matrix products, shards(): jnp.einsum('kl,mkab->mlab', level_mix, spread.astype(jnp.bfloat16), prefe...  50 us
    add x2, other arithmetic, taps_along(): summed = summed + weights[position] * piece.astype(jnp.float32)  43.7 us
    unnamed x22, local copies, waits for them, and re-layouts  36.8 us
    slice x4, local copies, waits for them, and re-layouts, with_halo(): last = lax.slice_in_dim(shard, length - width, length, axis=dim)  28.6 us
    slice x4, local copies, waits for them, and re-layouts, with_halo(): leading = lax.slice_in_dim(shard, 0, width, axis=dim)  26.7 us
    reduce_sum x1, other arithmetic, shards(): increment = jnp.sum(ensemble.astype(jnp.float32) * localized, axis=0)  23 us
  transfers between devices with their start and end apart: 8, of which 2 were waited for; matrix products, arithmetic and copies ran while one was open for 13% of the time, Pallas kernels for 0%

profile of v1, /device:TPU:1, one launch (start us, length us, event | category | flops | bytes accessed | tf_op | source)
XLA Modules:
  0.0 535.7 jit_solution(218320749881276664)
XLA Ops:
  1.3 6.3 %convert_bitcast_fusion = bf16[80,32,8,128]{3,1,2,0:T(8,128)(2,1)} fusion(bf16[80,32,8,128]{3,2,1,0:T(8,128)(2,1)} %param.10, bf16[32,32]{1,0:T(8,128)(2,1)S(1)} %copy-done), kind=kOutput, calls=%fused_computation.59 | convolution fusion | flops 170393600 | bytes 10487808 | tf_op jit(solution)/shard_map/kl,mlab->mkab/dot_general | solution.py:44
  7.7 11.1 %fusion.50 = (bf16[80,32,8,2]{3,1,2,0:T(8,128)(2,1)}, bf16[80,32,8,2]{3,1,2,0:T(8,128)(2,1)}) fusion(bf16[80,32,8,128]{3,1,2,0:T(8,128)(2,1)} %convert_bitcast_fusion), kind=kLoop, calls=%fused_computation.92 | loop fusion | bytes 327680 | tf_op jit(solution)/shard_map/slice | solution.py:14
  18.8 7.6 %copy.55 = bf16[80,32,8,2]{0,2,3,1:T(8,128)(2,1)S(1)} copy(bf16[80,32,8,2]{3,1,2,0:T(8,128)(2,1)} %get-tuple-element.17) | data formatting | bytes 163840 | tf_op jit(solution)/shard_map/slice | solution.py:15
  28.3 7.5 %copy.53 = bf16[80,32,8,2]{0,2,3,1:T(8,128)(2,1)S(1)} copy(bf16[80,32,8,2]{3,1,2,0:T(8,128)(2,1)} %get-tuple-element.16) | data formatting | bytes 163840 | tf_op jit(solution)/shard_map/slice | solution.py:14
  41.6 9.3 %copy.56 = bf16[80,32,8,2]{3,1,2,0:T(8,128)(2,1)} copy(bf16[80,32,8,2]{0,2,3,1:T(8,128)(2,1)S(1)} %collective-permute-done.1) | data formatting | bytes 163840 | tf_op jit(solution)/shard_map/ppermute | solution.py:17
  50.8 9.3 %copy.54 = bf16[80,32,8,2]{3,1,2,0:T(8,128)(2,1)} copy(bf16[80,32,8,2]{0,2,3,1:T(8,128)(2,1)S(1)} %collective-permute-done) | data formatting | bytes 163840 | tf_op jit(solution)/shard_map/ppermute | solution.py:16
  60.1 30.0 %multiply_add_fusion.1 = f32[80,32,8,128]{3,1,2,0:T(8,128)S(1)} fusion(bf16[80,32,8,128]{3,1,2,0:T(8,128)(2,1)} %convert_bitcast_fusion, bf16[80,32,8,2]{3,1,2,0:T(8,128)(2,1)} %copy.56, bf16[80,32,8,2]{3,1,2,0:T(8,128)(2,1)} %copy.54, f32[]{:T(128)} %bitcast.11, f32[]{:T(128)} %bitcast.10, f32[]{:T(128)} %bitcast.9, f32[]{:T(128)} %bitcast.8), kind=kLoop, calls=%fused_computation.46 | loop fusion | flops 65536000 | bytes 15892496 | tf_op jit(solution)/shard_map/add | solution.py:27
  101.8 10.7 %copy.64 = bf16[80,32,8,128]{0,3,2,1:T(8,128)(2,1)} copy(bf16[80,32,8,128]{3,2,1,0:T(8,128)(2,1)} %param.11) | data formatting | bytes 10485760 | tf_op args[1]
  112.5 10.1 %gather_fusion.1 = bf16[2048,80]{1,0:T(8,128)(2,1)S(1)} fusion(bf16[80,32768]{0,1:T(8,128)(2,1)} %bitcast.43, s32[2048]{0:T(1024)S(1)} %broadcast_clamp_fusion), kind=kCustom, calls=%fused_computation.1 | custom fusion | bytes 663552 | tf_op jit(solution)/shard_map/gather | solution.py:70
  123.2 87.8 %collective-permute-done.3 = f32[80,32,2,128]{3,1,2,0:T(8,128)} collective-permute-done((f32[80,32,2,128]{3,1,2,0:T(8,128)}, f32[80,32,2,128]{3,1,2,0:T(8,128)}, u32[]{:S(2)}, u32[]{:S(2)}) %collective-permute-start.3) | collective-permute-done | bytes 2621472 | tf_op jit(solution)/shard_map/ppermute | solution.py:17
  211.7 23.0 %fusion = f32[32,8,128]{2,0,1:T(8,128)S(1)} fusion(f32[80,32,8,128]{3,1,2,0:T(8,128)} %copy-done.2, f32[80,32,2,128]{3,1,2,0:T(8,128)} %collective-permute-done.3, f32[80,32,2,128]{3,1,2,0:T(8,128)} %collective-permute-done.2, f32[]{:T(128)} %bitcast.15, f32[]{:T(128)} %bitcast.14, f32[]{:T(128)} %bitcast.13, f32[]{:T(128)} %bitcast.12, ...), kind=kLoop, calls=%fused_computation.13 | loop fusion | flops 39288832 | bytes 21102608 | tf_op jit(solution)/shard_map/reduce_sum | solution.py:51
  234.8 11.8 %gather_fusion = f32[2048]{0:T(1024)S(1)} fusion(f32[32768]{0:T(1024)S(1)} %bitcast.42, s32[2048]{0:T(1024)S(1)} %broadcast_clamp_fusion), kind=kCustom, calls=%fused_computation | custom fusion | bytes 24576 | tf_op jit(solution)/shard_map/gather | solution.py:59
  246.6 11.3 %scatter_custom_fusion = f32[32768]{0:T(1024)S(1)} fusion(s32[2048]{0:T(1024)S(1)} %bitcast.48, f32[2048]{0:T(1024)S(1)} %get-tuple-element.19, f32[]{:T(128)} %constant.39.clone.1), kind=kCustom, calls=%fused_computation.68 | custom fusion | flops 2048 | bytes 131076 | tf_op jit(solution)/shard_map/scatter-add | solution.py:60
  273.7 115.9 %all-gather = f32[2560,80]{1,0:T(8,128)S(1)} all-gather(f32[80,80]{1,0:T(8,128)S(1)} %fusion.35), channel_id=2, replica_groups=mesh['lat'=4,'lon'=8] {'lat','lon'}, dimensions={0}, use_global_device_ids=true | all-gather | bytes 844800 | tf_op jit(solution)/shard_map/all_gather | solution.py:76
  389.9 7.3 %cholesky.20 = f32[80,80]{1,0:T(8,128)S(1)} custom-call(f32[80,80]{1,0:T(8,128)S(1)} %fusion.42), custom_call_target="Cholesky" | custom-call | tf_op jit(solution)/shard_map/jit(cholesky)/cholesky | solution.py:77
  398.1 13.7 %multiply_add_fusion = f32[80,32,8,128]{3,1,2,0:T(8,128)S(1)} fusion(bf16[80,32,8,128]{3,1,2,0:T(8,128)(2,1)} %copy-done.3, bf16[80,32,2,128]{3,1,2,0:T(8,128)(2,1)S(1)} %collective-permute-done.5, bf16[80,32,2,128]{3,1,2,0:T(8,128)(2,1)} %collective-permute-done.4, f32[]{:T(128)} %bitcast.15, f32[]{:T(128)} %bitcast.14, f32[]{:T(128)} %bitcast.13, f32[]{:T(128)} %bitcast.12), kind=kLoop, calls=%fused_computation.45 | loop fusion | flops 44564480 | bytes 18350096 | tf_op jit(solution)/shard_map/add | solution.py:27
  411.7 9.6 %fusion.47 = (f32[80,32,8,2]{3,1,2,0:T(8,128)}, f32[80,32,8,2]{3,1,2,0:T(8,128)}) fusion(f32[80,32,8,128]{3,1,2,0:T(8,128)S(1)} %multiply_add_fusion), kind=kLoop, calls=%fused_computation.89 | loop fusion | bytes 655360 | tf_op jit(solution)/shard_map/slice | solution.py:15
  422.0 7.5 %copy.61 = f32[80,32,8,2]{0,2,3,1:T(8,128)S(1)} copy(f32[80,32,8,2]{3,1,2,0:T(8,128)} %get-tuple-element.11) | data formatting | bytes 327680 | tf_op jit(solution)/shard_map/slice | solution.py:14
  429.5 8.1 %collective-permute-start.7 = (f32[80,32,8,2]{0,2,3,1:T(8,128)S(1)}, f32[80,32,8,2]{0,2,3,1:T(8,128)S(1)}, u32[]{:S(2)}, u32[]{:S(2)}) collective-permute-start(f32[80,32,8,2]{0,2,3,1:T(8,128)S(1)} %copy.61), channel_id=1, source_target_pairs={{0,8},{8,16},{16,24},{1,9},{9,17},{17,25},{2,10},{10,18},{18,26},{... | collective-permute-start | bytes 491528 | tf_op jit(solution)/shard_map/ppermute | solution.py:16
  437.6 7.5 %copy.59 = f32[80,32,8,2]{0,2,3,1:T(8,128)S(1)} copy(f32[80,32,8,2]{3,1,2,0:T(8,128)} %get-tuple-element.10) | data formatting | bytes 327680 | tf_op jit(solution)/shard_map/slice | solution.py:15
  448.4 9.1 %copy.62 = f32[80,32,8,2]{3,1,2,0:T(8,128)} copy(f32[80,32,8,2]{0,2,3,1:T(8,128)S(1)} %collective-permute-done.7) | data formatting | bytes 327680 | tf_op jit(solution)/shard_map/ppermute | solution.py:16
  457.6 9.2 %copy.60 = f32[80,32,8,2]{3,1,2,0:T(8,128)} copy(f32[80,32,8,2]{0,2,3,1:T(8,128)S(1)} %collective-permute-done.6) | data formatting | bytes 327680 | tf_op jit(solution)/shard_map/ppermute | solution.py:17
  466.8 50.0 %bitcast_add_fusion = f32[80,32,8,128]{3,1,2,0:T(8,128)} fusion(bf16[80,32,8,128]{3,2,1,0:T(8,128)(2,1)} %param.10, f32[80,32,8,2]{3,1,2,0:T(8,128)} %copy.62, f32[80,32,8,128]{3,1,2,0:T(8,128)} %copy-done.1, f32[80,32,8,2]{3,1,2,0:T(8,128)} %copy.60, f32[]{:T(128)} %bitcast.11, f32[]{:T(128)} %bitcast.10, f32[]{:T(128)} %bitcast.9, f32[]{:T(128)} %bitcast.8, ...), kind=kOutput, calls=%fused_computation.44 | convolution fusion | flops 207093760 | bytes 26544144 | tf_op jit(solution)/shard_map/kl,mkab->mlab/dot_general | solution.py:66
  516.8 18.3 %copy.69 = f32[80,32,8,128]{3,2,1,0:T(8,128)} copy(f32[80,32,8,128]{3,1,2,0:T(8,128)} %bitcast_add_fusion) | data formatting | bytes 20971520
  (55 shorter events, 41.5 us)
Async XLA Ops:
  0.6 0.7 copy-start
  18.8 22.1 %copy-start.8 = (f32[4]{0:T(128)S(1)}, f32[4]{0:T(128)}, u32[]{:S(2)}) copy-start(f32[4]{0:T(128)} %param.13) | copy-start | bytes 52
  26.4 15.2 %collective-permute-start.1 = (bf16[80,32,8,2]{0,2,3,1:T(8,128)(2,1)S(1)}, bf16[80,32,8,2]{0,2,3,1:T(8,128)(2,1)S(1)}, u32[]{:S(2)}, u32[]{:S(2)}) collective-permute-start(bf16[80,32,8,2]{0,2,3,1:T(8,128)(2,1)S(1)} %copy.55), channel_id=1, source_target_pairs={{8,0},{16,8},{24,16},{9,1},{17,9},{25,17},{10,2},{18,10},{26,18},{... | collective-permute-start | bytes 245768 | tf_op jit(solution)/shard_map/ppermute | solution.py:17
  35.9 15.0 %collective-permute-start = (bf16[80,32,8,2]{0,2,3,1:T(8,128)(2,1)S(1)}, bf16[80,32,8,2]{0,2,3,1:T(8,128)(2,1)S(1)}, u32[]{:S(2)}, u32[]{:S(2)}) collective-permute-start(bf16[80,32,8,2]{0,2,3,1:T(8,128)(2,1)S(1)} %copy.53), channel_id=1, source_target_pairs={{0,8},{8,16},{16,24},{1,9},{9,17},{17,25},{2,10},{10,18},{18,26},{... | collective-permute-start | bytes 245768 | tf_op jit(solution)/shard_map/ppermute | solution.py:16
  90.2 4.1 copy-start.2
  94.3 6.9 %copy-start.6 = (s32[1,1,2048]{2,1,0:T(1,128)S(1)}, s32[1,1,2048]{2,1,0:T(1,128)}, u32[]{:S(2)}) copy-start(s32[1,1,2048]{2,1,0:T(1,128)} %param.17) | copy-start | bytes 24580
  94.3 18.2 %copy-start.7 = (s32[1,1,2048]{2,1,0:T(1,128)S(1)}, s32[1,1,2048]{2,1,0:T(1,128)}, u32[]{:S(2)}) copy-start(s32[1,1,2048]{2,1,0:T(1,128)} %param.15) | copy-start | bytes 24580
  96.7 25.9 %copy-start.9 = (f32[4]{0:T(128)S(1)}, f32[4]{0:T(128)}, u32[]{:S(2)}) copy-start(f32[4]{0:T(128)} %param.14) | copy-start | bytes 52
  96.7 114.4 %collective-permute-start.3 = (f32[80,32,2,128]{3,1,2,0:T(8,128)}, f32[80,32,2,128]{3,1,2,0:T(8,128)}, u32[]{:S(2)}, u32[]{:S(2)}) collective-permute-start(f32[80,32,2,128]{3,1,2,0:T(8,128)} %get-tuple-element.13), channel_id=1, source_target_pairs={{1,0},{2,1},{3,2},{4,3},{5,4},{6,5},{7,6},{0,7},{9,8},{10,9},{11,1... | collective-permute-start | bytes 7864328 | tf_op jit(solution)/shard_map/ppermute | solution.py:17
  100.9 110.8 %collective-permute-start.2 = (f32[80,32,2,128]{3,1,2,0:T(8,128)S(1)}, f32[80,32,2,128]{3,1,2,0:T(8,128)}, u32[]{:S(2)}, u32[]{:S(2)}) collective-permute-start(f32[80,32,2,128]{3,1,2,0:T(8,128)S(1)} %get-tuple-element.12), channel_id=1, source_target_pairs={{0,1},{1,2},{2,3},{3,4},{4,5},{5,6},{6,7},{7,0},{8,9},{9,10},{10,1... | collective-permute-start | bytes 7864328 | tf_op jit(solution)/shard_map/ppermute | solution.py:16
  211.7 34.9 %copy-start.4 = (f32[1,1,2048]{2,1,0:T(1,128)S(1)}, f32[1,1,2048]{2,1,0:T(1,128)}, u32[]{:S(2)}) copy-start(f32[1,1,2048]{2,1,0:T(1,128)} %param.19) | copy-start | bytes 24580
  211.7 34.9 %copy-start.5 = (f32[1,1,2048]{2,1,0:T(1,128)S(1)}, f32[1,1,2048]{2,1,0:T(1,128)}, u32[]{:S(2)}) copy-start(f32[1,1,2048]{2,1,0:T(1,128)} %param.18) | copy-start | bytes 24580
  262.2 2.4 copy-start.3
  266.6 131.4 %collective-permute-start.5 = (bf16[80,32,2,128]{3,1,2,0:T(8,128)(2,1)}, bf16[80,32,2,128]{3,1,2,0:T(8,128)(2,1)S(1)}, u32[]{:S(2)}, u32[]{:S(2)}) collective-permute-start(bf16[80,32,2,128]{3,1,2,0:T(8,128)(2,1)} %get-tuple-element.15), channel_id=1, source_target_pairs={{0,1},{1,2},{2,3},{3,4},{4,5},{5,6},{6,7},{7,0},{8,9},{9,10},{10,1... | collective-permute-start | bytes 3932168 | tf_op jit(solution)/shard_map/ppermute | solution.py:16
  268.9 129.2 %collective-permute-start.4 = (bf16[80,32,2,128]{3,1,2,0:T(8,128)(2,1)}, bf16[80,32,2,128]{3,1,2,0:T(8,128)(2,1)}, u32[]{:S(2)}, u32[]{:S(2)}) collective-permute-start(bf16[80,32,2,128]{3,1,2,0:T(8,128)(2,1)} %get-tuple-element.14), channel_id=1, source_target_pairs={{1,0},{2,1},{3,2},{4,3},{5,4},{6,5},{7,6},{0,7},{9,8},{10,9},{11,1... | collective-permute-start | bytes 3932168 | tf_op jit(solution)/shard_map/ppermute | solution.py:17
  411.7 10.2 %copy-start.1 = (f32[80,32,8,128]{3,1,2,0:T(8,128)}, f32[80,32,8,128]{3,1,2,0:T(8,128)S(1)}, u32[]{:S(2)}) copy-start(f32[80,32,8,128]{3,1,2,0:T(8,128)S(1)} %multiply_add_fusion) | copy-start | bytes 31457284
  429.5 19.0 %collective-permute-start.7 = (f32[80,32,8,2]{0,2,3,1:T(8,128)S(1)}, f32[80,32,8,2]{0,2,3,1:T(8,128)S(1)}, u32[]{:S(2)}, u32[]{:S(2)}) collective-permute-start(f32[80,32,8,2]{0,2,3,1:T(8,128)S(1)} %copy.61), channel_id=1, source_target_pairs={{0,8},{8,16},{16,24},{1,9},{9,17},{17,25},{2,10},{10,18},{18,26},{... | collective-permute-start | bytes 491528 | tf_op jit(solution)/shard_map/ppermute | solution.py:16
  445.1 12.5 %collective-permute-start.6 = (f32[80,32,8,2]{0,2,3,1:T(8,128)S(1)}, f32[80,32,8,2]{0,2,3,1:T(8,128)S(1)}, u32[]{:S(2)}, u32[]{:S(2)}) collective-permute-start(f32[80,32,8,2]{0,2,3,1:T(8,128)S(1)} %copy.59), channel_id=1, source_target_pairs={{8,0},{16,8},{24,16},{9,1},{17,9},{25,17},{10,2},{18,10},{26,18},{... | collective-permute-start | bytes 491528 | tf_op jit(solution)/shard_map/ppermute | solution.py:17
